TPU v7x, 512 devices: a whole 4x4x16 slice. The times are simulated.
512 devices in a mesh: leaf: 128 (over z, y, core), rep: 4 (over x).
Axes of the slice: x: 4, y: 4, z: 16, core: 2. Of those that a mesh axis runs over, the one named last changes fastest.
Arguments:
- positions: float32 [3, 8192, 128], P(None, ('leaf', 'rep')), may hold values from -6 to 6
- density: float32 [3, 8192, 128], P(None, ('leaf', 'rep')), may hold values from -6 to 6
- near_offset: int32 [8192, 12], P(('leaf', 'rep')), may hold values from -2 to 2
- near_count: int32 [8192], P(('leaf', 'rep')), may hold values from 1 to 12
- inter_list: int32 [512, 189], P(('leaf', 'rep')), may hold values from 0 to 511
- operator_index: int32 [512, 189], P(('leaf', 'rep')), may hold values from 0 to 3
- lattice_index: int32 [512], P(('leaf', 'rep')), may hold values from 0 to 1
- up_weight: bfloat16 [512, 384], replicated, may hold values from -0.3125 to 0.3125
- m2l_operators: bfloat16 [4, 512, 512], replicated, may hold values from -0.0390625 to 0.0390625
- lattice_operators: bfloat16 [2, 512, 512], replicated, may hold values from -0.01171875 to 0.01171875
- down_weight: bfloat16 [384, 512], replicated, may hold values from -0.5 to 0.5
Outputs:
- velocity: float32 [3, 8192, 128], P(None, ('leaf', 'rep'))
Inputs may be any that keep to these rules, and one draw needn't show every extreme that they name: `near_offset`: leaf g's near source leaves are (g + offset) mod 8192; slots at or past near_count are unused.
All inputs are finite; a program needn't handle non-finite values.
Results may differ from a plain program's by a relative error of at most 0.02.
Values may be sent and summed in bfloat16 or wider, within the bound.
A program may use at most 64 MiB of HBM per device.

v0:
```python
import math
import jax
import jax.numpy as jnp
from jax import lax
from jax.sharding import PartitionSpec as P


def padded(shard, sides, width):
    for axis, dim in sides:
        size, length = (lax.axis_size(axis), shard.shape[dim])
        up = [(i, (i + 1) % size) for i in range(size)]
        down = [(j, i) for i, j in up]
        last = lax.slice_in_dim(shard, length - width, length, axis=dim)
        first = lax.slice_in_dim(shard, 0, width, axis=dim)
        before = lax.ppermute(last, axis, up)
        after = lax.ppermute(first, axis, down)
        shard = jnp.concatenate([before, shard, after], axis=dim)
    return shard


def stokes_tile(target, source_pos, source_force, live_slots):
    offsets_xyz = target[:, None, :, None] - source_pos[:, :, None, :]
    distance_sq = jnp.sum(offsets_xyz * offsets_xyz, axis=0) + 0.05
    inverse = lax.rsqrt(distance_sq)
    inverse_cube = inverse * inverse * inverse
    projected = jnp.sum(offsets_xyz * source_force[:, :, None, :], axis=0)
    kernel_terms = source_force[:, :, None, :] * inverse + offsets_xyz * (projected * inverse_cube)
    kernel_terms = kernel_terms * live_slots[None, :, None, None]
    return jnp.sum(kernel_terms, axis=(1, 3)) * (1.0 / (8.0 * math.pi))


def body(
    positions,
    density,
    near_offset,
    near_count,
    inter_list,
    operator_index,
    lattice_index,
    up_weight,
    m2l_operators,
    lattice_operators,
    down_weight,
):
    per_box = positions.shape[1]
    node_count = positions.shape[2]
    kind_count = m2l_operators.shape[0]
    stacked = jnp.concatenate([positions, density], axis=0)
    extended = padded(stacked.astype(jnp.bfloat16), ((("leaf", "rep"), 1),), per_box).astype(
        stacked.dtype
    )
    slot_range = jnp.arange(near_offset.shape[1], dtype=jnp.int32)

    def one_leaf(leaf_slot):
        target = positions[:, leaf_slot]
        source_slot = leaf_slot + near_offset[leaf_slot] + per_box
        sources = jnp.take(extended, source_slot, axis=1)
        live_slots = (slot_range < near_count[leaf_slot]).astype(jnp.float32)
        return stokes_tile(target, sources[:3], sources[3:], live_slots)

    near_part = lax.map(one_leaf, jnp.arange(per_box, dtype=jnp.int32))
    near_part = jnp.transpose(near_part, (1, 0, 2))
    damping = 1.0 / (1.0 + jnp.sum(positions * positions, axis=0))
    summed = jnp.sum(density * damping[None], axis=1).reshape(-1).astype(jnp.bfloat16)
    coarse = jnp.dot(up_weight, summed, preferred_element_type=jnp.float32).astype(jnp.bfloat16)
    coarse_row = coarse.reshape(1, -1)
    box_ids = inter_list[0]
    op_kinds = operator_index[0]
    kind_range = jnp.arange(kind_count, dtype=jnp.int32)
    selector = (op_kinds[None, :] == kind_range[:, None]).astype(jnp.float32)
    all_blocks = lax.all_gather(coarse_row, ("leaf", "rep"), axis=0, tiled=True)
    chosen = jnp.take(all_blocks, box_ids, axis=0).astype(jnp.float32)
    grouped_sum = jnp.dot(selector, chosen, precision=lax.Precision.HIGHEST)
    block_sum = jnp.sum(all_blocks.astype(jnp.float32), axis=0)
    block_sum = lax.psum(coarse.astype(jnp.float32), ("leaf", "rep"))
    total = block_sum.astype(jnp.bfloat16)
    grouped = grouped_sum.astype(jnp.bfloat16)
    local = jnp.einsum("tij,tj->i", m2l_operators, grouped, preferred_element_type=jnp.float32)
    local = local + jnp.dot(
        lattice_operators[lattice_index[0]], total, preferred_element_type=jnp.float32
    )
    local_bf = local.astype(jnp.bfloat16)
    far_part = jnp.dot(down_weight, local_bf, preferred_element_type=jnp.float32).reshape(
        3, node_count
    )
    return near_part + damping[None] * far_part[:, None, :]


def solution(mesh):
    in_specs = (
        P(None, ("leaf", "rep"), None),
        P(None, ("leaf", "rep"), None),
        P(("leaf", "rep"), None),
        P(("leaf", "rep")),
        P(("leaf", "rep"), None),
        P(("leaf", "rep"), None),
        P(("leaf", "rep")),
        P(),
        P(),
        P(),
        P(),
    )
    out_specs = P(None, ("leaf", "rep"), None)
    return jax.shard_map(body, mesh=mesh, in_specs=in_specs, out_specs=out_specs, check_vma=False)
```

profile of v0, /device:TPU:4, one launch (start us, length us, event | category | flops | bytes accessed | tf_op | source)
XLA Modules:
  0.0 417.0 jit_solution(9846070013614672958)
XLA Ops:
  1.8 3.1 collective-permute-start
  4.9 2.7 collective-permute-start.1
  8.9 108.3 %psum.7 = bf16[512]{0:T(512)(128)(2,1)S(1)} all-reduce(bf16[512]{0:T(512)(128)(2,1)S(1)} %convert_element_type.40), channel_id=1, replica_groups=mesh['leaf'=128,'rep'=4] {'leaf','rep'}, use_global_device_ids=true, to_apply=%region_7.8 | all-reduce | flops 512 | bytes 2048 | tf_op jit(solution)/shard_map/psum | solution.py:75
  117.8 136.1 %all-gather.1 = bf16[512,1,512]{2,1,0:T(2,128)(2,1)S(1)} all-gather(bf16[1,1,512]{2,1,0:T(2,128)(2,1)S(1)} %reshape.142), channel_id=2, replica_groups=mesh['leaf'=128,'rep'=4] {'leaf','rep'}, dimensions={0}, use_global_device_ids=true | all-gather | bytes 525312 | tf_op jit(solution)/shard_map/all_gather | solution.py:71
  257.8 158.6 %while.13 = (s32[]{:T(128)}, f32[16,3,128]{2,0,1:T(8,128)S(1)}, s32[16]{0:T(128)S(1)}, s32[16,12]{1,0:T(8,128)}, f32[6,48,128]{2,0,1:T(8,128)S(1)}, /*index=5*/f...) while((s32[]{:T(128)}, f32[16,3,128]{2,0,1:T(8,128)S(1)}, ...), condition=%wide.region_4.5_spmd.clone, body=%wide.region_0.4_spmd.clone.sunk | while | flops 6891705 | bytes 6684707 | solution.py:61
  260.5 1.4 fusion.33
  262.5 1.4 compare_and_fusion.3
  270.4 1.4 fusion.33
  272.4 1.4 compare_and_fusion.3
  280.3 1.4 fusion.33
  282.3 1.4 compare_and_fusion.3
  290.3 1.4 fusion.33
  292.2 1.4 compare_and_fusion.3
  300.2 1.4 fusion.33
  302.1 1.4 compare_and_fusion.3
  310.1 1.4 fusion.33
  312.0 1.4 compare_and_fusion.3
  320.0 1.4 fusion.33
  322.0 1.4 compare_and_fusion.3
  329.9 1.4 fusion.33
  331.9 1.4 compare_and_fusion.3
  339.8 1.4 fusion.33
  341.8 1.4 compare_and_fusion.3
  349.7 1.4 fusion.33
  351.7 1.4 compare_and_fusion.3
  359.6 1.4 fusion.33
  361.6 1.4 compare_and_fusion.3
  371.5 1.4 compare_and_fusion.3
  381.4 1.4 compare_and_fusion.3
  391.3 1.4 compare_and_fusion.3
  401.3 1.4 compare_and_fusion.3
  411.2 1.4 compare_and_fusion.3
  (314 shorter events, 93.6 us)
Async XLA Ops:
  0.0 255.4 %copy-start = (bf16[4,512,512]{2,1,0:T(8,128)(2,1)S(1)}, bf16[4,512,512]{2,1,0:T(8,128)(2,1)}, u32[]{:S(2)}) copy-start(bf16[4,512,512]{2,1,0:T(8,128)(2,1)} %param.21) | copy-start | bytes 6291460
  0.0 254.1 %copy-start.2 = (s32[1,189]{1,0:T(1,128)S(1)}, s32[1,189]{1,0:T(1,128)}, u32[]{:S(2)}) copy-start(s32[1,189]{1,0:T(1,128)} %param.17) | copy-start | bytes 2272
  1.8 255.9 %collective-permute-start = (bf16[6,16,128]{2,1,0:T(8,128)(2,1)S(1)}, bf16[6,16,128]{2,1,0:T(8,128)(2,1)S(1)}, u32[]{:S(2)}, u32[]{:S(2)}) collective-permute-start(bf16[6,16,128]{2,1,0:T(8,128)(2,1)S(1)} %pad_maximum_fusion), channel_id=1, source_target_pairs={{0,1},{1,2},{2,3},{3,4},{4,5},{5,6},{6,7},{7,8},{8,9},{9,10},{10,1... | collective-permute-start | bytes 73736 | tf_op jit(solution)/shard_map/ppermute | solution.py:15
  4.9 252.8 %collective-permute-start.1 = (bf16[6,16,128]{2,1,0:T(8,128)(2,1)S(1)}, bf16[6,16,128]{2,1,0:T(8,128)(2,1)S(1)}, u32[]{:S(2)}, u32[]{:S(2)}) collective-permute-start(bf16[6,16,128]{2,1,0:T(8,128)(2,1)S(1)} %pad_maximum_fusion), channel_id=1, source_target_pairs={{1,0},{2,1},{3,2},{4,3},{5,4},{6,5},{7,6},{8,7},{9,8},{10,9},{11,1... | collective-permute-start | bytes 73736 | tf_op jit(solution)/shard_map/ppermute | solution.py:16
  117.8 137.4 %copy-start.3 = (s32[1,189]{1,0:T(1,128)S(1)}, s32[1,189]{1,0:T(1,128)}, u32[]{:S(2)}) copy-start(s32[1,189]{1,0:T(1,128)} %param.18) | copy-start | bytes 2272
  254.1 3.2 copy-start.1
  255.2 2.6 copy-start.4
where the time goes:
time: 420 us; the launch traced here: 417 us
  blocking collectives  244 us (58%)
  other arithmetic  83.3 us (20%)
  local copies, waits for them, and re-layouts  44.2 us (11%)
  loops' own time  34.7 us (8%)
  starting transfers between devices  5.84 us (1%)
    all_gather x1, blocking collectives, body(): all_blocks = lax.all_gather(coarse_row, ('leaf', 'rep'), axis=0, tiled=True)  136 us
    psum x1, blocking collectives, body(): block_sum = lax.psum(coarse.astype(jnp.float32), ('leaf', 'rep'))  108 us
    another operation x1, loops' own time, body(): near_part = lax.map(one_leaf, jnp.arange(per_box, dtype=jnp.int32))  34.7 us
    select_n x32, other arithmetic, one_leaf(): sources = jnp.take(extended, source_slot, axis=1)  23.5 us
    and x16, other arithmetic, one_leaf(): sources = jnp.take(extended, source_slot, axis=1)  22.2 us
    dynamic_slice x32, local copies, waits for them, and re-layouts, one_leaf(): target = positions[:, leaf_slot]  11.6 us
    convert_element_type x16, other arithmetic, one_leaf(): live_slots = (slot_range < near_count[leaf_slot]).astype(jnp.float32)  11 us
    reduce_sum x16, other arithmetic, stokes_tile(): return jnp.sum(kernel_terms, axis=(1, 3)) * (1.0 / (8.0 * math.pi))  10.7 us
  transfers between devices with their start and end apart: 2, of which 0 were waited for; matrix products, arithmetic and copies ran while one was open for 1% of the time, Pallas kernels for 0%

commit v1 on v0

--- a/solution.py
+++ b/solution.py
@@ -72,7 +72,7 @@
     chosen = jnp.take(all_blocks, box_ids, axis=0).astype(jnp.float32)
     grouped_sum = jnp.dot(selector, chosen, precision=lax.Precision.HIGHEST)
     block_sum = jnp.sum(all_blocks.astype(jnp.float32), axis=0)
-    block_sum = lax.psum(coarse.astype(jnp.float32), ("leaf", "rep"))
+    block_sum = lax.psum(lax.psum(coarse.astype(jnp.float32), "rep"), "leaf")
     total = block_sum.astype(jnp.bfloat16)
     grouped = grouped_sum.astype(jnp.bfloat16)
     local = jnp.einsum("tij,tj->i", m2l_operators, grouped, preferred_element_type=jnp.float32)

time: 420 us -> 576 us (1.37)
  the two profiles are of different devices: /device:TPU:4 before, /device:TPU:2 now
where the time goes in v1:
time: 576 us; the launch traced here: 573 us
  blocking collectives  396 us (69%)
  other arithmetic  83.3 us (14%)
  local copies, waits for them, and re-layouts  44.2 us (8%)
  loops' own time  34.7 us (6%)
  starting transfers between devices  9.74 us (2%)
    psum x2, blocking collectives, body(): block_sum = lax.psum(lax.psum(coarse.astype(jnp.float32), 'rep'), 'leaf')  263 us
    all_gather x1, blocking collectives, body(): all_blocks = lax.all_gather(coarse_row, ('leaf', 'rep'), axis=0, tiled=True)  134 us
    another operation x1, loops' own time, body(): near_part = lax.map(one_leaf, jnp.arange(per_box, dtype=jnp.int32))  34.7 us
    select_n x32, other arithmetic, one_leaf(): sources = jnp.take(extended, source_slot, axis=1)  23.5 us
    and x16, other arithmetic, one_leaf(): sources = jnp.take(extended, source_slot, axis=1)  22.2 us
    dynamic_slice x32, local copies, waits for them, and re-layouts, one_leaf(): target = positions[:, leaf_slot]  11.6 us
  transfers between devices with their start and end apart: 2, of which 0 were waited for; matrix products, arithmetic and copies ran while one was open for 1% of the time, Pallas kernels for 0%

profile of v1, /device:TPU:2, one launch (start us, length us, event | category | flops | bytes accessed | tf_op | source)
XLA Modules:
  0.0 572.9 jit_solution(17631662634200828836)
XLA Ops:
  1.8 3.4 collective-permute-start
  5.2 6.3 %collective-permute-start.1 = (bf16[6,16,128]{2,1,0:T(8,128)(2,1)S(1)}, bf16[6,16,128]{2,1,0:T(8,128)(2,1)S(1)}, u32[]{:S(2)}, u32[]{:S(2)}) collective-permute-start(bf16[6,16,128]{2,1,0:T(8,128)(2,1)S(1)} %pad_maximum_fusion), channel_id=1, source_target_pairs={{1,0},{2,1},{3,2},{4,3},{5,4},{6,5},{7,6},{8,7},{9,8},{10,9},{11,1... | collective-permute-start | bytes 73736 | tf_op jit(solution)/shard_map/ppermute | solution.py:16
  12.7 15.9 %psum.14 = f32[512]{0:T(512)S(1)} all-reduce(bf16[512]{0:T(512)(128)(2,1)S(1)} %convert_element_type.40), channel_id=1, replica_groups=mesh['leaf'=128,'rep'=4] {'rep'}, use_global_device_ids=true, to_apply=%region_7.8 | all-reduce | flops 512 | bytes 3072 | tf_op jit(solution)/shard_map/psum | solution.py:75
  29.3 246.8 %psum.15 = bf16[512]{0:T(512)(128)(2,1)S(1)} all-reduce(f32[512]{0:T(512)S(1)} %psum.14), channel_id=1, replica_groups=mesh['leaf'=128,'rep'=4] {'leaf'}, use_global_device_ids=true, to_apply=%region_8.9 | all-reduce | flops 512 | bytes 3072 | tf_op jit(solution)/shard_map/psum | solution.py:75
  276.2 133.7 %all-gather.1 = bf16[512,1,512]{2,1,0:T(2,128)(2,1)S(1)} all-gather(bf16[1,1,512]{2,1,0:T(2,128)(2,1)S(1)} %reshape.142), channel_id=2, replica_groups=mesh['leaf'=128,'rep'=4] {'leaf','rep'}, dimensions={0}, use_global_device_ids=true | all-gather | bytes 525312 | tf_op jit(solution)/shard_map/all_gather | solution.py:71
  413.7 158.6 %while.13 = (s32[]{:T(128)}, f32[16,3,128]{2,0,1:T(8,128)S(1)}, s32[16]{0:T(128)S(1)}, s32[16,12]{1,0:T(8,128)}, f32[6,48,128]{2,0,1:T(8,128)S(1)}, /*index=5*/f...) while((s32[]{:T(128)}, f32[16,3,128]{2,0,1:T(8,128)S(1)}, ...), condition=%wide.region_4.5_spmd.clone, body=%wide.region_0.4_spmd.clone.sunk | while | flops 6891705 | bytes 6684707 | solution.py:61
  416.4 1.4 fusion.33
  418.4 1.4 compare_and_fusion.3
  426.3 1.4 fusion.33
  428.3 1.4 compare_and_fusion.3
  436.3 1.4 fusion.33
  438.2 1.4 compare_and_fusion.3
  446.2 1.4 fusion.33
  448.1 1.4 compare_and_fusion.3
  456.1 1.4 fusion.33
  458.0 1.4 compare_and_fusion.3
  466.0 1.4 fusion.33
  467.9 1.4 compare_and_fusion.3
  475.9 1.4 fusion.33
  477.9 1.4 compare_and_fusion.3
  485.8 1.4 fusion.33
  487.8 1.4 compare_and_fusion.3
  495.7 1.4 fusion.33
  497.7 1.4 compare_and_fusion.3
  507.6 1.4 compare_and_fusion.3
  517.5 1.4 compare_and_fusion.3
  527.4 1.4 compare_and_fusion.3
  537.3 1.4 compare_and_fusion.3
  545.3 1.4 fusion.33
  547.3 1.4 compare_and_fusion.3
  557.2 1.4 compare_and_fusion.3
  567.1 1.4 compare_and_fusion.3
  (315 shorter events, 95.0 us)
Async XLA Ops:
  0.0 411.3 %copy-start = (bf16[4,512,512]{2,1,0:T(8,128)(2,1)S(1)}, bf16[4,512,512]{2,1,0:T(8,128)(2,1)}, u32[]{:S(2)}) copy-start(bf16[4,512,512]{2,1,0:T(8,128)(2,1)} %param.21) | copy-start | bytes 6291460
  0.0 410.0 %copy-start.2 = (s32[1,189]{1,0:T(1,128)S(1)}, s32[1,189]{1,0:T(1,128)}, u32[]{:S(2)}) copy-start(s32[1,189]{1,0:T(1,128)} %param.17) | copy-start | bytes 2272
  1.8 411.8 %collective-permute-start = (bf16[6,16,128]{2,1,0:T(8,128)(2,1)S(1)}, bf16[6,16,128]{2,1,0:T(8,128)(2,1)S(1)}, u32[]{:S(2)}, u32[]{:S(2)}) collective-permute-start(bf16[6,16,128]{2,1,0:T(8,128)(2,1)S(1)} %pad_maximum_fusion), channel_id=1, source_target_pairs={{0,1},{1,2},{2,3},{3,4},{4,5},{5,6},{6,7},{7,8},{8,9},{9,10},{10,1... | collective-permute-start | bytes 73736 | tf_op jit(solution)/shard_map/ppermute | solution.py:15
  5.2 408.4 %collective-permute-start.1 = (bf16[6,16,128]{2,1,0:T(8,128)(2,1)S(1)}, bf16[6,16,128]{2,1,0:T(8,128)(2,1)S(1)}, u32[]{:S(2)}, u32[]{:S(2)}) collective-permute-start(bf16[6,16,128]{2,1,0:T(8,128)(2,1)S(1)} %pad_maximum_fusion), channel_id=1, source_target_pairs={{1,0},{2,1},{3,2},{4,3},{5,4},{6,5},{7,6},{8,7},{9,8},{10,9},{11,1... | collective-permute-start | bytes 73736 | tf_op jit(solution)/shard_map/ppermute | solution.py:16
  276.2 134.9 %copy-start.3 = (s32[1,189]{1,0:T(1,128)S(1)}, s32[1,189]{1,0:T(1,128)}, u32[]{:S(2)}) copy-start(s32[1,189]{1,0:T(1,128)} %param.18) | copy-start | bytes 2272
  410.1 3.2 copy-start.1
  411.1 2.6 copy-start.4
